TPU v7x, 32 devices: a whole 2x2x4 slice. The times are simulated.
32 devices in a mesh: dp: 16 (over z, y, x), mp: 2 (over core).
Axes of the slice: x: 2, y: 2, z: 4, core: 2. Of those that a mesh axis runs over, the one named last changes fastest.
Arguments:
- store_rows: bfloat16 [8192, 4096], P('dp', 'mp'), may hold values from -64 to 64
- norm_gain: bfloat16 [4096], replicated, may hold values from 0.099609375 to 1.8984375
- key_weight: bfloat16 [4096, 2048], P(None, 'mp'), may hold values from -0.09375 to 0.09375
- value_weight: bfloat16 [4096, 2048], P(None, 'mp'), may hold values from -0.09375 to 0.09375
- queries: bfloat16 [128, 2048], P('dp', 'mp'), may hold values from -300 to 300
- counts: int32 [16], replicated, may hold values from 1 to 8, 32 in all
- slot_plan: int32 [32], P('dp'), may hold values from 0 to 31, each once
Outputs:
- context: bfloat16 [128, 2048], P('dp', 'mp')
All inputs are finite; a program needn't handle non-finite values.
Results may differ from a plain program's by a relative error of at most 0.0091.
Values may be sent and summed in bfloat16 or wider, within the bound.
A program may use at most 64 MiB of HBM per device.

v0:
```python
import jax
import jax.numpy as jnp
from jax import lax
from jax.sharding import PartitionSpec as P

HEAD_DIM = 64
norm_eps = 1e-06
score_scale = 0.125
far_below = -1e30


def local(store_rows, norm_gain, key_weight, value_weight, queries, counts, slot_plan):
    full_width = norm_gain.shape[0]
    row_count = store_rows.shape[0]
    local_cols = store_rows.shape[1]
    head_cols = key_weight.shape[1]
    heads_here = head_cols // HEAD_DIM
    passages_here = slot_plan.shape[0]
    seq_len = row_count // passages_here
    gain_full = norm_gain.astype(jnp.float32)
    raw_rows = store_rows.astype(jnp.float32)
    own_gain = lax.dynamic_slice_in_dim(gain_full, lax.axis_index("mp") * local_cols, local_cols, 0)
    scaled = (raw_rows * own_gain[None, :]).astype(jnp.bfloat16)
    total_sq = lax.psum(jnp.sum(raw_rows * raw_rows, axis=1), "mp")
    shard_part = lax.all_gather(scaled, "mp", axis=1, tiled=True)
    key_acc = jnp.dot(shard_part, key_weight, preferred_element_type=jnp.float32)
    value_acc = jnp.dot(shard_part, value_weight, preferred_element_type=jnp.float32)
    inv_rms = lax.rsqrt(total_sq / full_width + norm_eps)
    key_rows = (key_acc * inv_rms[:, None]).astype(jnp.bfloat16)
    value_rows = (value_acc * inv_rms[:, None]).astype(jnp.bfloat16)
    ends = jnp.cumsum(counts)
    slot_question = jnp.sum((slot_plan[:, None] >= ends[None, :]).astype(jnp.int32), axis=1)
    num_questions = counts.shape[0]
    dec_len = queries.shape[0]
    gathered = lax.all_gather(queries, "dp", axis=0, tiled=True)
    query_table = gathered.reshape(num_questions, dec_len, heads_here, HEAD_DIM)
    slot_queries = jnp.take(query_table, slot_question, axis=0)
    key_blocks = key_rows.reshape(passages_here, seq_len, heads_here, HEAD_DIM)
    value_blocks = value_rows.reshape(passages_here, seq_len, heads_here, HEAD_DIM).astype(
        jnp.float32
    )
    scores = (
        jnp.einsum("pihd,pthd->piht", slot_queries, key_blocks, preferred_element_type=jnp.float32)
        * score_scale
    )
    slot_max = jnp.max(scores, axis=3)
    member = slot_question[None, :] == jnp.arange(num_questions, dtype=jnp.int32)[:, None]
    member_float = member.astype(jnp.float32)
    question_max = jnp.max(jnp.where(member[:, :, None, None], slot_max[None], far_below), axis=1)
    max_level = lax.pmax(question_max, "dp")
    slot_level = jnp.take(max_level, slot_question, axis=0)
    weights = jnp.exp(scores - slot_level[..., None])
    slot_den = jnp.sum(weights, axis=3)
    slot_num = jnp.einsum("piht,pthd->pihd", weights, value_blocks, precision=lax.Precision.HIGHEST)
    slot_num = slot_num.reshape(passages_here, dec_len, head_cols)
    numerator = jnp.einsum("qp,pik->qik", member_float, slot_num, precision=lax.Precision.HIGHEST)
    denominator = jnp.einsum("qp,pih->qih", member_float, slot_den, precision=lax.Precision.HIGHEST)
    numerator, denominator = (numerator, denominator)
    summed_num, summed_den = (
        lax.psum_scatter(numerator, "dp", scatter_dimension=0, tiled=True),
        lax.psum_scatter(denominator, "dp", scatter_dimension=0, tiled=True),
    )
    own_num = summed_num[0]
    own_den = summed_den[0]
    context = own_num.reshape(dec_len, heads_here, HEAD_DIM) / own_den[..., None]
    return context.reshape(dec_len, head_cols).astype(jnp.bfloat16)


def solution(mesh):
    placed = (P("dp", "mp"), P(), P(None, "mp"), P(None, "mp"), P("dp", "mp"), P(), P("dp"))
    return jax.shard_map(
        local, mesh=mesh, in_specs=placed, out_specs=P("dp", "mp"), check_vma=False
    )
```

profile of v0, /device:TPU:0, one launch (start us, length us, event | category | flops | bytes accessed | tf_op | source)
XLA Modules:
  0.0 241.7 jit_solution(15678639214267508043)
XLA Ops:
  6.5 0.7 dynamic-slice_convert_fusion
  7.2 3.5 %fusion.1 = (f32[512]{0:T(512)S(1)}, bf16[512,2048]{1,0:T(8,128)(2,1)}) fusion(bf16[512,2048]{1,0:T(8,128)(2,1)} %param.7, f32[2048]{0:T(1024)S(1)} %dynamic-slice_convert_fusion), kind=kLoop, calls=%fused_computation.5 | loop fusion | flops 5242368 | bytes 4204544 | tf_op jit(solution)/shard_map/reduce_sum | solution.py:24
  10.8 0.6 copy-done.1
  11.4 0.1 copy.36
  11.5 0.1 reduce
  11.7 0.2 fusion.23
  11.8 0.1 iota_compare_fusion
  11.9 0.1 copy.41
  12.0 43.8 %all_gather.7 = bf16[128,1024]{1,0:T(8,128)(2,1)S(1)} all-gather(bf16[8,1024]{1,0:T(8,128)(2,1)S(1)} %copy-done), channel_id=1, replica_groups=mesh['dp'=16,'mp'=2] {'dp'}, dimensions={0}, use_global_device_ids=true | all-gather | bytes 278528 | tf_op jit(solution)/shard_map/all_gather | solution.py:35
  55.8 0.3 reshape.86
  56.2 0.6 gather_fusion
  56.7 2.5 %psum.7 = f32[512]{0:T(512)S(1)} all-reduce(f32[512]{0:T(512)S(1)} %get-tuple-element.5), channel_id=1, replica_groups=mesh['dp'=16,'mp'=2] {'mp'}, use_global_device_ids=true, to_apply=%region_3.4 | all-reduce | flops 512 | bytes 4096 | tf_op jit(solution)/shard_map/psum | solution.py:24
  59.2 0.1 broadcast_select_fusion
  59.3 9.1 %multiply_convert_fusion.1 = bf16[512,1024]{1,0:T(8,128)(2,1)S(1)} fusion(bf16[512,4096]{1,0:T(8,128)(2,1)} %all-gather.2.cloned.1.call-done, bf16[4096,1024]{1,0:T(8,128)(2,1)} %param.10, f32[512]{0:T(512)S(1)} %add_rsqrt_fusion), kind=kOutput, calls=%fused_computation.11 | convolution fusion | flops 4296015872 | bytes 13633536 | tf_op jit(solution)/shard_map/dot_general | solution.py:27
  68.4 1.3 reshape.105
  69.8 9.1 %multiply_convert_fusion = bf16[512,1024]{1,0:T(8,128)(2,1)S(1)} fusion(bf16[512,4096]{1,0:T(8,128)(2,1)} %all-gather.2.cloned.1.call-done, bf16[4096,1024]{1,0:T(8,128)(2,1)} %param.9, f32[512]{0:T(512)S(1)} %add_rsqrt_fusion), kind=kOutput, calls=%fused_computation.10 | convolution fusion | flops 4296015872 | bytes 13633536 | tf_op jit(solution)/shard_map/dot_general | solution.py:26
  78.9 2.4 reshape.106
  81.3 2.3 fusion.25
  83.7 0.1 select_reduce_fusion
  83.8 72.0 %pmax.7 = f32[16,8,16]{2,1,0:T(8,128)S(1)} all-reduce(f32[16,8,16]{2,1,0:T(8,128)S(1)} %select_reduce_fusion), channel_id=1, replica_groups=mesh['dp'=16,'mp'=2] {'dp'}, use_global_device_ids=true, to_apply=%region_6.7 | all-reduce | flops 2048 | bytes 16384 | tf_op jit(solution)/shard_map/pmax | solution.py:50
  155.8 0.5 gather_fusion.1
  156.5 1.2 fusion.12
  157.8 0.1 reshape.107
  157.9 0.5 fusion.21
  158.4 1.1 copy.47
  159.5 0.6 dynamic-slice
  160.1 0.2 fusion.15
  160.4 0.3 fusion.19
  160.7 71.9 %all-reduce = f32[16,8,16]{2,1,0:T(8,128)S(1)} all-reduce(f32[16,8,16]{2,1,0:T(8,128)S(1)} %copy.49), channel_id=3, replica_groups=mesh['dp'=16,'mp'=2] {'dp'}, use_global_device_ids=true, to_apply=%region_9.10.clone | all-reduce | flops 2048 | bytes 16384
  232.7 0.6 dynamic-slice_bitcast_fusion
  233.4 0.1 div.23
  233.5 1.4 fusion.18
  (25 shorter events, 0.6 us)
Async XLA Ops:
  6.5 52.8 %all-gather.2.cloned.1.call-start = ((), (), s32[]{:S(2)}) async-start(), calls=%async_computation.1 | async-start | bytes 6291456 | tf_op jit(solution)/shard_map/all_gather | solution.py:25
  10.8 0.7 copy-start.1
  10.8 0.9 copy-start.2
  10.8 1.3 copy-start
  10.8 222.7 %reduce-scatter.2.cloned.1.call-start = ((), (), s32[]{:S(2)}) async-start(), calls=%async_computation.2 | async-start | bytes 557056 | tf_op jit(solution)/shard_map/reduce_scatter | solution.py:60
  157.7 1.8 copy-start.3
Sparse Core Ops, SparseCore 0:
  10.9 16.3 all-gather.1
  159.6 72.4 reduce-scatter.1
where the time goes:
time: 242 us
  blocking collectives  190 us (79%)
  matrix products  22.6 us (9%)
  between operations  13.6 us (6%)
  local copies, waits for them, and re-layouts  8.82 us (4%)
  other arithmetic  6.49 us (3%)
    pmax x1, blocking collectives, local(): max_level = lax.pmax(question_max, 'dp')  72 us
    unnamed x1, blocking collectives  71.9 us
    all_gather x1, blocking collectives, local(): gathered = lax.all_gather(queries, 'dp', axis=0, tiled=True)  43.8 us
    dot_general x1, matrix products, local(): jnp.dot(shard_part, key_weight, preferred_element_type=jnp.float32)  9.15 us
    dot_general x1, matrix products, local(): jnp.dot(shard_part, value_weight, preferred_element_type=jnp.float32)  9.15 us
  transfers between devices with their start and end apart: 2, of which 0 were waited for; matrix products, arithmetic and copies ran while one was open for 1% of the time, Pallas kernels for 0%

commit v1 on v0

--- a/solution.py
+++ b/solution.py
@@ -32,7 +32,21 @@
     slot_question = jnp.sum((slot_plan[:, None] >= ends[None, :]).astype(jnp.int32), axis=1)
     num_questions = counts.shape[0]
     dec_len = queries.shape[0]
-    gathered = lax.all_gather(queries, "dp", axis=0, tiled=True)
+    ways, here, step = (lax.axis_size("dp"), lax.axis_index("dp"), queries.shape[0])
+    shape = [n * ways if d == 0 else n for d, n in enumerate(queries.shape)]
+    full = lax.dynamic_update_slice_in_dim(
+        jnp.zeros(shape, queries.dtype), queries, here * step, axis=0
+    )
+    going_up = going_down = queries
+    for far in range(1, ways // 2 + 1):
+        going_up = lax.ppermute(going_up, "dp", [(d, (d + 1) % ways) for d in range(ways)])
+        full = lax.dynamic_update_slice_in_dim(full, going_up, (here - far) % ways * step, axis=0)
+        if 2 * far < ways:
+            going_down = lax.ppermute(going_down, "dp", [(d, (d - 1) % ways) for d in range(ways)])
+            full = lax.dynamic_update_slice_in_dim(
+                full, going_down, (here + far) % ways * step, axis=0
+            )
+    gathered = full
     query_table = gathered.reshape(num_questions, dec_len, heads_here, HEAD_DIM)
     slot_queries = jnp.take(query_table, slot_question, axis=0)
     key_blocks = key_rows.reshape(passages_here, seq_len, heads_here, HEAD_DIM)

time: 242 us -> 263 us (1.087)
  blocking collectives: 190 us -> 146 us
  starting transfers between devices: 0.04 us -> 42.1 us
  waiting for transfers between devices: 0.05 us -> 21.8 us
    all_gather x1 -> x0, blocking collectives: 43.8 us -> none  [local(): gathered = lax.all_gather(queries, 'dp', axis=0, tiled=True)]
    ppermute x0 -> x15, starting transfers between devices: none -> 42.1 us  [the longest x7 42.1 us: local(): lax.ppermute(going_down, 'dp', [(d, (d - 1) % ways) for d in range(ways)])]
    ppermute x0 -> x15, waiting for transfers between devices: none -> 21.7 us  [the longest x8 14.6 us: local(): lax.ppermute(going_up, 'dp', [(d, (d + 1) % ways) for d in range(ways)])]
  transfers between devices with their start and end apart: 2 -> 17, of which waited for: 0 -> 7; matrix products, arithmetic and copies ran while one was open for 1% -> 1% of each run, Pallas kernels for 0% -> 0%
where the time goes in v1:
time: 263 us; the launch traced here: 262 us
  blocking collectives  146 us (56%)
  starting transfers between devices  42.1 us (16%)
  matrix products  22.6 us (9%)
  waiting for transfers between devices  21.8 us (8%)
  between operations  13.9 us (5%)
  local copies, waits for them, and re-layouts  9 us (3%)
  other arithmetic  6.48 us (2%)
    pmax x1, blocking collectives, local(): max_level = lax.pmax(question_max, 'dp')  72 us
    unnamed x1, blocking collectives  71.9 us
    ppermute x7, starting transfers between devices, local(): lax.ppermute(going_down, 'dp', [(d, (d - 1) % ways) for d in range(ways)])  42.1 us
    ppermute x8, waiting for transfers between devices, local(): lax.ppermute(going_up, 'dp', [(d, (d + 1) % ways) for d in range(ways)])  14.6 us
    dot_general x1, matrix products, local(): jnp.dot(shard_part, key_weight, preferred_element_type=jnp.float32)  9.15 us
    dot_general x1, matrix products, local(): jnp.dot(shard_part, value_weight, preferred_element_type=jnp.float32)  9.15 us
    ppermute x7, waiting for transfers between devices, local(): lax.ppermute(going_down, 'dp', [(d, (d - 1) % ways) for d in range(ways)])  7.08 us
  transfers between devices with their start and end apart: 17, of which 7 were waited for; matrix products, arithmetic and copies ran while one was open for 1% of the time, Pallas kernels for 0%

profile of v1, /device:TPU:0, one launch (start us, length us, event | category | flops | bytes accessed | tf_op | source)
XLA Modules:
  0.0 262.3 jit_solution(3879171532434962550)
XLA Ops:
  6.5 0.7 dynamic-slice_convert_fusion
  7.2 3.5 %fusion.1 = (f32[512]{0:T(512)S(1)}, bf16[512,2048]{1,0:T(8,128)(2,1)}) fusion(bf16[512,2048]{1,0:T(8,128)(2,1)} %param.7, f32[2048]{0:T(1024)S(1)} %dynamic-slice_convert_fusion), kind=kLoop, calls=%fused_computation.5 | loop fusion | flops 5242368 | bytes 4204544 | tf_op jit(solution)/shard_map/reduce_sum | solution.py:24
  10.8 0.6 copy-done
  11.5 6.9 %collective-permute-start.1 = (bf16[8,1024]{1,0:T(8,128)(2,1)S(1)}, bf16[8,1024]{1,0:T(8,128)(2,1)S(1)}, u32[]{:S(2)}, u32[]{:S(2)}) collective-permute-start(bf16[8,1024]{1,0:T(8,128)(2,1)S(1)} %copy-done), channel_id=1, source_target_pairs={{0,30},{2,0},{4,2},{6,4},{8,6},{10,8},{12,10},{14,12},{16,14},{18,... | collective-permute-start | bytes 49160 | tf_op jit(solution)/shard_map/ppermute | solution.py:45
  18.6 2.5 psum.7
  21.8 5.7 %collective-permute-start.3 = (bf16[8,1024]{1,0:T(8,128)(2,1)S(1)}, bf16[8,1024]{1,0:T(8,128)(2,1)S(1)}, u32[]{:S(2)}, u32[]{:S(2)}) collective-permute-start(bf16[8,1024]{1,0:T(8,128)(2,1)S(1)} %collective-permute-done.1), channel_id=1, source_target_pairs={{0,30},{2,0},{4,2},{6,4},{8,6},{10,8},{12,10},{14,12},{16,14},{18,... | collective-permute-start | bytes 49160 | tf_op jit(solution)/shard_map/ppermute | solution.py:45
  27.5 1.4 collective-permute-done.3
  28.9 5.9 %collective-permute-start.5 = (bf16[8,1024]{1,0:T(8,128)(2,1)S(1)}, bf16[8,1024]{1,0:T(8,128)(2,1)S(1)}, u32[]{:S(2)}, u32[]{:S(2)}) collective-permute-start(bf16[8,1024]{1,0:T(8,128)(2,1)S(1)} %collective-permute-done.3), channel_id=1, source_target_pairs={{0,30},{2,0},{4,2},{6,4},{8,6},{10,8},{12,10},{14,12},{16,14},{18,... | collective-permute-start | bytes 49160 | tf_op jit(solution)/shard_map/ppermute | solution.py:45
  34.9 1.4 collective-permute-done.5
  36.3 5.9 %collective-permute-start.7 = (bf16[8,1024]{1,0:T(8,128)(2,1)S(1)}, bf16[8,1024]{1,0:T(8,128)(2,1)S(1)}, u32[]{:S(2)}, u32[]{:S(2)}) collective-permute-start(bf16[8,1024]{1,0:T(8,128)(2,1)S(1)} %collective-permute-done.5), channel_id=1, source_target_pairs={{0,30},{2,0},{4,2},{6,4},{8,6},{10,8},{12,10},{14,12},{16,14},{18,... | collective-permute-start | bytes 49160 | tf_op jit(solution)/shard_map/ppermute | solution.py:45
  42.2 1.4 collective-permute-done.7
  43.6 5.9 %collective-permute-start.9 = (bf16[8,1024]{1,0:T(8,128)(2,1)S(1)}, bf16[8,1024]{1,0:T(8,128)(2,1)S(1)}, u32[]{:S(2)}, u32[]{:S(2)}) collective-permute-start(bf16[8,1024]{1,0:T(8,128)(2,1)S(1)} %collective-permute-done.7), channel_id=1, source_target_pairs={{0,30},{2,0},{4,2},{6,4},{8,6},{10,8},{12,10},{14,12},{16,14},{18,... | collective-permute-start | bytes 49160 | tf_op jit(solution)/shard_map/ppermute | solution.py:45
  49.5 1.4 collective-permute-done.9
  50.9 5.9 %collective-permute-start.11 = (bf16[8,1024]{1,0:T(8,128)(2,1)S(1)}, bf16[8,1024]{1,0:T(8,128)(2,1)S(1)}, u32[]{:S(2)}, u32[]{:S(2)}) collective-permute-start(bf16[8,1024]{1,0:T(8,128)(2,1)S(1)} %collective-permute-done.9), channel_id=1, source_target_pairs={{0,30},{2,0},{4,2},{6,4},{8,6},{10,8},{12,10},{14,12},{16,14},{18,... | collective-permute-start | bytes 49160 | tf_op jit(solution)/shard_map/ppermute | solution.py:45
  56.9 1.4 collective-permute-done.11
  58.3 5.9 %collective-permute-start.13 = (bf16[8,1024]{1,0:T(8,128)(2,1)S(1)}, bf16[8,1024]{1,0:T(8,128)(2,1)S(1)}, u32[]{:S(2)}, u32[]{:S(2)}) collective-permute-start(bf16[8,1024]{1,0:T(8,128)(2,1)S(1)} %collective-permute-done.11), channel_id=1, source_target_pairs={{0,30},{2,0},{4,2},{6,4},{8,6},{10,8},{12,10},{14,12},{16,14},{18,... | collective-permute-start | bytes 49160 | tf_op jit(solution)/shard_map/ppermute | solution.py:45
  64.2 7.3 %collective-permute-done.12 = bf16[8,1024]{1,0:T(8,128)(2,1)S(1)} collective-permute-done((bf16[8,1024]{1,0:T(8,128)(2,1)S(1)}, bf16[8,1024]{1,0:T(8,128)(2,1)S(1)}, u32[]{:S(2)}, u32[]{:S(2)}) %collective-permute-start.12) | collective-permute-done | bytes 16416 | tf_op jit(solution)/shard_map/ppermute | solution.py:42
  71.5 7.3 %collective-permute-done.14 = bf16[8,1024]{1,0:T(8,128)(2,1)S(1)} collective-permute-done((bf16[8,1024]{1,0:T(8,128)(2,1)S(1)}, bf16[8,1024]{1,0:T(8,128)(2,1)S(1)}, u32[]{:S(2)}, u32[]{:S(2)}) %collective-permute-start.14) | collective-permute-done | bytes 16416 | tf_op jit(solution)/shard_map/ppermute | solution.py:42
  79.2 0.6 gather_fusion
  79.8 9.1 %multiply_convert_fusion.1 = bf16[512,1024]{1,0:T(8,128)(2,1)S(1)} fusion(bf16[512,4096]{1,0:T(8,128)(2,1)} %all-gather.2.cloned.1.call-done, bf16[4096,1024]{1,0:T(8,128)(2,1)} %param.10, f32[512]{0:T(512)S(1)} %add_rsqrt_fusion), kind=kOutput, calls=%fused_computation.11 | convolution fusion | flops 4296015872 | bytes 13633536 | tf_op jit(solution)/shard_map/dot_general | solution.py:27
  89.0 1.3 reshape.105
  90.3 9.1 %multiply_convert_fusion = bf16[512,1024]{1,0:T(8,128)(2,1)S(1)} fusion(bf16[512,4096]{1,0:T(8,128)(2,1)} %all-gather.2.cloned.1.call-done, bf16[4096,1024]{1,0:T(8,128)(2,1)} %param.9, f32[512]{0:T(512)S(1)} %add_rsqrt_fusion), kind=kOutput, calls=%fused_computation.10 | convolution fusion | flops 4296015872 | bytes 13633536 | tf_op jit(solution)/shard_map/dot_general | solution.py:26
  99.5 2.4 reshape.106
  101.9 2.3 fusion.25
  104.4 72.0 %pmax.7 = f32[16,8,16]{2,1,0:T(8,128)S(1)} all-reduce(f32[16,8,16]{2,1,0:T(8,128)S(1)} %select_reduce_fusion), channel_id=1, replica_groups=mesh['dp'=16,'mp'=2] {'dp'}, use_global_device_ids=true, to_apply=%region_6.7 | all-reduce | flops 2048 | bytes 16384 | tf_op jit(solution)/shard_map/pmax | solution.py:64
  176.4 0.5 gather_fusion.1
  177.1 1.2 fusion.12
  179.0 1.1 copy.47
  180.1 0.6 dynamic-slice
  181.3 71.9 %all-reduce = f32[16,8,16]{2,1,0:T(8,128)S(1)} all-reduce(f32[16,8,16]{2,1,0:T(8,128)S(1)} %copy.49), channel_id=3, replica_groups=mesh['dp'=16,'mp'=2] {'dp'}, use_global_device_ids=true, to_apply=%region_9.10.clone | all-reduce | flops 2048 | bytes 16384
  253.2 0.6 dynamic-slice_bitcast_fusion
  254.1 1.4 fusion.18
  (71 shorter events, 3.1 us)
Async XLA Ops:
  6.5 73.3 %all-gather.2.cloned.1.call-start = ((), (), s32[]{:S(2)}) async-start(), calls=%async_computation.1 | async-start | bytes 6291456 | tf_op jit(solution)/shard_map/all_gather | solution.py:25
  10.7 0.7 copy-start
  10.8 7.7 %copy-start.1 = (s32[16]{0:T(128)S(1)}, s32[16]{0:T(128)}, u32[]{:S(2)}) copy-start(s32[16]{0:T(128)} %param.12) | copy-start | bytes 196
  10.8 10.4 %copy-start.2 = (s32[2]{0:T(128)S(1)}, s32[2]{0:T(128)}, u32[]{:S(2)}) copy-start(s32[2]{0:T(128)} %param.13) | copy-start | bytes 28
  10.8 243.3 %reduce-scatter.2.cloned.1.call-start = ((), (), s32[]{:S(2)}) async-start(), calls=%async_computation.2 | async-start | bytes 557056 | tf_op jit(solution)/shard_map/reduce_scatter | solution.py:74
  11.5 10.3 %collective-permute-start.1 = (bf16[8,1024]{1,0:T(8,128)(2,1)S(1)}, bf16[8,1024]{1,0:T(8,128)(2,1)S(1)}, u32[]{:S(2)}, u32[]{:S(2)}) collective-permute-start(bf16[8,1024]{1,0:T(8,128)(2,1)S(1)} %copy-done), channel_id=1, source_target_pairs={{0,30},{2,0},{4,2},{6,4},{8,6},{10,8},{12,10},{14,12},{16,14},{18,... | collective-permute-start | bytes 49160 | tf_op jit(solution)/shard_map/ppermute | solution.py:45
  18.4 9.1 %collective-permute-start = (bf16[8,1024]{1,0:T(8,128)(2,1)S(1)}, bf16[8,1024]{1,0:T(8,128)(2,1)S(1)}, u32[]{:S(2)}, u32[]{:S(2)}) collective-permute-start(bf16[8,1024]{1,0:T(8,128)(2,1)S(1)} %copy-done), channel_id=1, source_target_pairs={{0,2},{2,4},{4,6},{6,8},{8,10},{10,12},{12,14},{14,16},{16,18},{18... | collective-permute-start | bytes 49160 | tf_op jit(solution)/shard_map/ppermute | solution.py:42
  21.8 7.1 %collective-permute-start.3 = (bf16[8,1024]{1,0:T(8,128)(2,1)S(1)}, bf16[8,1024]{1,0:T(8,128)(2,1)S(1)}, u32[]{:S(2)}, u32[]{:S(2)}) collective-permute-start(bf16[8,1024]{1,0:T(8,128)(2,1)S(1)} %collective-permute-done.1), channel_id=1, source_target_pairs={{0,30},{2,0},{4,2},{6,4},{8,6},{10,8},{12,10},{14,12},{16,14},{18,... | collective-permute-start | bytes 49160 | tf_op jit(solution)/shard_map/ppermute | solution.py:45
  27.5 7.3 %collective-permute-start.2 = (bf16[8,1024]{1,0:T(8,128)(2,1)S(1)}, bf16[8,1024]{1,0:T(8,128)(2,1)S(1)}, u32[]{:S(2)}, u32[]{:S(2)}) collective-permute-start(bf16[8,1024]{1,0:T(8,128)(2,1)S(1)} %collective-permute-done), channel_id=1, source_target_pairs={{0,2},{2,4},{4,6},{6,8},{8,10},{10,12},{12,14},{14,16},{16,18},{18... | collective-permute-start | bytes 49160 | tf_op jit(solution)/shard_map/ppermute | solution.py:42
  28.9 7.3 %collective-permute-start.5 = (bf16[8,1024]{1,0:T(8,128)(2,1)S(1)}, bf16[8,1024]{1,0:T(8,128)(2,1)S(1)}, u32[]{:S(2)}, u32[]{:S(2)}) collective-permute-start(bf16[8,1024]{1,0:T(8,128)(2,1)S(1)} %collective-permute-done.3), channel_id=1, source_target_pairs={{0,30},{2,0},{4,2},{6,4},{8,6},{10,8},{12,10},{14,12},{16,14},{18,... | collective-permute-start | bytes 49160 | tf_op jit(solution)/shard_map/ppermute | solution.py:45
  34.8 7.3 %collective-permute-start.4 = (bf16[8,1024]{1,0:T(8,128)(2,1)S(1)}, bf16[8,1024]{1,0:T(8,128)(2,1)S(1)}, u32[]{:S(2)}, u32[]{:S(2)}) collective-permute-start(bf16[8,1024]{1,0:T(8,128)(2,1)S(1)} %collective-permute-done.2), channel_id=1, source_target_pairs={{0,2},{2,4},{4,6},{6,8},{8,10},{10,12},{12,14},{14,16},{16,18},{18... | collective-permute-start | bytes 49160 | tf_op jit(solution)/shard_map/ppermute | solution.py:42
  36.3 7.3 %collective-permute-start.7 = (bf16[8,1024]{1,0:T(8,128)(2,1)S(1)}, bf16[8,1024]{1,0:T(8,128)(2,1)S(1)}, u32[]{:S(2)}, u32[]{:S(2)}) collective-permute-start(bf16[8,1024]{1,0:T(8,128)(2,1)S(1)} %collective-permute-done.5), channel_id=1, source_target_pairs={{0,30},{2,0},{4,2},{6,4},{8,6},{10,8},{12,10},{14,12},{16,14},{18,... | collective-permute-start | bytes 49160 | tf_op jit(solution)/shard_map/ppermute | solution.py:45
  42.2 7.3 %collective-permute-start.6 = (bf16[8,1024]{1,0:T(8,128)(2,1)S(1)}, bf16[8,1024]{1,0:T(8,128)(2,1)S(1)}, u32[]{:S(2)}, u32[]{:S(2)}) collective-permute-start(bf16[8,1024]{1,0:T(8,128)(2,1)S(1)} %collective-permute-done.4), channel_id=1, source_target_pairs={{0,2},{2,4},{4,6},{6,8},{8,10},{10,12},{12,14},{14,16},{16,18},{18... | collective-permute-start | bytes 49160 | tf_op jit(solution)/shard_map/ppermute | solution.py:42
  43.6 7.3 %collective-permute-start.9 = (bf16[8,1024]{1,0:T(8,128)(2,1)S(1)}, bf16[8,1024]{1,0:T(8,128)(2,1)S(1)}, u32[]{:S(2)}, u32[]{:S(2)}) collective-permute-start(bf16[8,1024]{1,0:T(8,128)(2,1)S(1)} %collective-permute-done.7), channel_id=1, source_target_pairs={{0,30},{2,0},{4,2},{6,4},{8,6},{10,8},{12,10},{14,12},{16,14},{18,... | collective-permute-start | bytes 49160 | tf_op jit(solution)/shard_map/ppermute | solution.py:45
  49.5 7.3 %collective-permute-start.8 = (bf16[8,1024]{1,0:T(8,128)(2,1)S(1)}, bf16[8,1024]{1,0:T(8,128)(2,1)S(1)}, u32[]{:S(2)}, u32[]{:S(2)}) collective-permute-start(bf16[8,1024]{1,0:T(8,128)(2,1)S(1)} %collective-permute-done.6), channel_id=1, source_target_pairs={{0,2},{2,4},{4,6},{6,8},{8,10},{10,12},{12,14},{14,16},{16,18},{18... | collective-permute-start | bytes 49160 | tf_op jit(solution)/shard_map/ppermute | solution.py:42
  50.9 7.3 %collective-permute-start.11 = (bf16[8,1024]{1,0:T(8,128)(2,1)S(1)}, bf16[8,1024]{1,0:T(8,128)(2,1)S(1)}, u32[]{:S(2)}, u32[]{:S(2)}) collective-permute-start(bf16[8,1024]{1,0:T(8,128)(2,1)S(1)} %collective-permute-done.9), channel_id=1, source_target_pairs={{0,30},{2,0},{4,2},{6,4},{8,6},{10,8},{12,10},{14,12},{16,14},{18,... | collective-permute-start | bytes 49160 | tf_op jit(solution)/shard_map/ppermute | solution.py:45
  56.8 7.3 %collective-permute-start.10 = (bf16[8,1024]{1,0:T(8,128)(2,1)S(1)}, bf16[8,1024]{1,0:T(8,128)(2,1)S(1)}, u32[]{:S(2)}, u32[]{:S(2)}) collective-permute-start(bf16[8,1024]{1,0:T(8,128)(2,1)S(1)} %collective-permute-done.8), channel_id=1, source_target_pairs={{0,2},{2,4},{4,6},{6,8},{8,10},{10,12},{12,14},{14,16},{16,18},{18... | collective-permute-start | bytes 49160 | tf_op jit(solution)/shard_map/ppermute | solution.py:42
  58.3 13.2 %collective-permute-start.13 = (bf16[8,1024]{1,0:T(8,128)(2,1)S(1)}, bf16[8,1024]{1,0:T(8,128)(2,1)S(1)}, u32[]{:S(2)}, u32[]{:S(2)}) collective-permute-start(bf16[8,1024]{1,0:T(8,128)(2,1)S(1)} %collective-permute-done.11), channel_id=1, source_target_pairs={{0,30},{2,0},{4,2},{6,4},{8,6},{10,8},{12,10},{14,12},{16,14},{18,... | collective-permute-start | bytes 49160 | tf_op jit(solution)/shard_map/ppermute | solution.py:45
  64.2 7.3 %collective-permute-start.12 = (bf16[8,1024]{1,0:T(8,128)(2,1)S(1)}, bf16[8,1024]{1,0:T(8,128)(2,1)S(1)}, u32[]{:S(2)}, u32[]{:S(2)}) collective-permute-start(bf16[8,1024]{1,0:T(8,128)(2,1)S(1)} %collective-permute-done.10), channel_id=1, source_target_pairs={{0,2},{2,4},{4,6},{6,8},{8,10},{10,12},{12,14},{14,16},{16,18},{18... | collective-permute-start | bytes 49160 | tf_op jit(solution)/shard_map/ppermute | solution.py:42
  71.5 7.3 %collective-permute-start.14 = (bf16[8,1024]{1,0:T(8,128)(2,1)S(1)}, bf16[8,1024]{1,0:T(8,128)(2,1)S(1)}, u32[]{:S(2)}, u32[]{:S(2)}) collective-permute-start(bf16[8,1024]{1,0:T(8,128)(2,1)S(1)} %collective-permute-done.12), channel_id=1, source_target_pairs={{0,2},{2,4},{4,6},{6,8},{8,10},{10,12},{12,14},{14,16},{16,18},{18... | collective-permute-start | bytes 49160 | tf_op jit(solution)/shard_map/ppermute | solution.py:42
  178.3 1.8 copy-start.3
Sparse Core Ops, SparseCore 0:
  10.9 16.3 all-gather.1
  180.2 72.4 reduce-scatter.1
